TPU v7x, 128 devices: a whole 4x4x4 slice. The times are simulated.
128 devices in a mesh: seq: 16 (over x, z), hx: 8 (over y, core).
Axes of the slice: x: 4, y: 4, z: 4, core: 2. Of those that a mesh axis runs over, the one named last changes fastest.
Arguments:
- query: bfloat16 [16384, 8192], P('seq', 'hx'), may hold values from -6 to 6
- key_in: bfloat16 [16384, 8192], P('seq', 'hx'), may hold values from -6 to 6
- value: bfloat16 [16384, 8192], P('seq', 'hx'), may hold values from -6 to 6
- head_gain: float32 [8192], P('hx'), may hold values from 0.1 to 1.9
- out_weight: bfloat16 [8192, 6144], P('hx', 'seq'), may hold values from -0.0625 to 0.0625
- residual: bfloat16 [16384, 6144], P(('seq', 'hx')), may hold values from -6 to 6
Outputs:
- mixed: bfloat16 [16384, 6144], P(('seq', 'hx'))
All inputs are finite; a program needn't handle non-finite values.
Results may differ from a plain program's by a relative error of at most 0.014.
Values may be sent and summed in bfloat16 or wider, within the bound.
No kernel may reach another device: no remote copies, remote signals or barrier semaphores. Data moves between devices by JAX's collectives and lax.ppermute only.
A program may use at most 128 MiB of HBM per device.

v0:
```python
import jax
import jax.numpy as jnp
from jax import lax
from jax.sharding import PartitionSpec as P

DH = 128


def activate(array):
    return jax.nn.silu(array.astype(jnp.float32)).astype(jnp.bfloat16)


def per_device(query, key_in, value, head_gain, out_weight, residual):
    highest = lax.Precision.HIGHEST
    tokens_here, width = query.shape
    heads = width // DH
    q_act = activate(query).reshape(tokens_here, heads, DH)
    k_act = activate(key_in).reshape(tokens_here, heads, DH)
    v_heads = value.reshape(tokens_here, heads, DH)
    blocks = min(512, tokens_here)
    count = tokens_here // blocks
    rows = jnp.arange(blocks, dtype=jnp.int32)
    lower = rows[:, None] >= rows[None, :]
    running = jnp.zeros((heads, DH, DH), jnp.float32)
    pieces = []
    for index in range(count):
        q_part = q_act[index * blocks : (index + 1) * blocks]
        k_part = k_act[index * blocks : (index + 1) * blocks]
        v_part = v_heads[index * blocks : (index + 1) * blocks]
        scores = jnp.einsum("thd,shd->hts", q_part, k_part, preferred_element_type=jnp.float32)
        scores = jnp.where(lower[None, :, :], scores, jnp.zeros_like(scores))
        inner = jnp.einsum("hts,she->the", scores, v_part.astype(jnp.float32), precision=highest)
        if index > 0:
            inner = inner + jnp.einsum(
                "thd,hde->the", q_part.astype(jnp.float32), running, precision=highest
            )
        pieces.append(inner)
        running = running + jnp.einsum(
            "thd,the->hde", k_part, v_part, preferred_element_type=jnp.float32
        )
    local_part = jnp.concatenate(pieces, axis=0)
    empty = jnp.zeros((heads, DH, DH), jnp.float32)
    position = lax.axis_index("seq")
    piece = lax.all_gather(running[None].astype(jnp.bfloat16), "seq", axis=0, tiled=True).astype(
        jnp.float32
    )
    ranks = jnp.arange(piece.shape[0], dtype=jnp.int32)
    keep = (ranks < position)[:, None, None, None]
    prefix = empty + jnp.sum(jnp.where(keep, piece, jnp.zeros_like(piece)), axis=0)
    attended = local_part + jnp.einsum(
        "thd,hde->the", q_act.astype(jnp.float32), prefix, precision=highest
    )
    meansq = jnp.mean(attended * attended, axis=-1, keepdims=True)
    normed = attended * lax.rsqrt(meansq + 1e-06) * head_gain.reshape(heads, DH)
    normed = normed.astype(jnp.bfloat16).reshape(tokens_here, width)
    full_weight = lax.all_gather(out_weight, "seq", axis=1, tiled=True)
    summed = lax.psum_scatter(
        jnp.dot(normed, full_weight, preferred_element_type=jnp.float32).astype(jnp.bfloat16),
        "hx",
        scatter_dimension=0,
        tiled=True,
    ).astype(jnp.float32)
    return (summed + residual.astype(jnp.float32)).astype(jnp.bfloat16)


def solution(mesh):
    return jax.shard_map(
        per_device,
        mesh=mesh,
        in_specs=(
            P("seq", "hx"),
            P("seq", "hx"),
            P("seq", "hx"),
            P("hx"),
            P("hx", "seq"),
            P(("seq", "hx"), None),
        ),
        out_specs=P(("seq", "hx"), None),
        check_vma=False,
    )
```

profile of v0, /device:TPU:1, one launch (start us, length us, event | category | flops | bytes accessed | tf_op | source)
XLA Modules:
  0.0 277.5 jit_solution(6667149055458355304)
XLA Ops:
  6.5 2.9 %copy.46 = bf16[1024,1024]{0,1:T(8,128)(2,1)S(1)} copy(bf16[1024,1024]{1,0:T(8,128)(2,1)} %param.7) | data formatting | bytes 4194304 | tf_op args[1]
  9.4 1.2 fusion.12
  10.6 1.1 fusion.25
  11.8 1.3 fusion.24
  13.1 0.5 copy.79
  13.6 1.9 copy.78
  15.5 0.4 fusion.28
  16.0 0.8 copy-done.7
  16.8 2.4 fusion.20
  19.2 0.0 all-gather.6.cloned.1.call-update
  19.2 0.0 all-gather.4.cloned.1.call-start
  19.2 0.7 all-gather.4.cloned.1.call-update
  19.9 0.0 reduce-scatter.2.cloned.1.call-start
  20.0 4.0 %copy.45 = bf16[1024,1024]{0,1:T(8,128)(2,1)} copy(bf16[1024,1024]{1,0:T(8,128)(2,1)} %param.6) | data formatting | bytes 4194304 | tf_op args[0]
  24.0 0.1 iota_compare_fusion
  24.1 2.9 %fusion.8 = bf16[1024,1024]{0,1:T(8,128)(2,1)S(1)} fusion(bf16[1024,1024]{0,1:T(8,128)(2,1)} %copy.45), kind=kLoop, calls=%fused_computation.14 | loop fusion | flops 6291456 | bytes 4194304 | tf_op jit(solution)/shard_map/convert_element_type | solution.py:10
  27.0 0.1 fusion.23
  27.1 1.3 fusion.27
  28.4 4.5 %fusion.1 = f32[8,512,128]{2,1,0:T(8,128)S(1)} fusion(bf16[512,8,128]{0,2,1:T(8,128)(2,1)S(1)} %bitcast.41, f32[8,512,512]{2,1,0:T(8,128)S(1)} %fusion.27, pred[512,512]{1,0:T(8,128)(4,1)S(1)} %iota_compare_fusion), kind=kOutput, calls=%fused_computation.3 | convolution fusion | flops 3223322624 | bytes 11796480 | tf_op jit(solution)/shard_map/hts,she->the/dot_general | solution.py:32
  33.0 2.5 bitcast_add_fusion
  35.5 1.3 fusion.26
  36.8 6.0 %fusion.17 = f32[512,8,128]{2,0,1:T(8,128)} fusion(bf16[512,8,128]{0,2,1:T(8,128)(2,1)S(1)} %bitcast.37, f32[8,512,512]{2,1,0:T(8,128)S(1)} %fusion.26, pred[512,512]{1,0:T(8,128)(4,1)S(1)} %iota_compare_fusion), kind=kOutput, calls=%fused_computation.28 | convolution fusion | flops 3223322624 | bytes 11796480 | tf_op jit(solution)/shard_map/hts,she->the/dot_general | solution.py:32
  42.8 31.4 %all-gather.6.cloned.1.call-done = bf16[128,128,128]{2,1,0:T(8,128)(2,1)} async-done(((bf16[8,128,128]{2,1,0:T(8,128)(2,1)}), bf16[128,128,128]{2,1,0:T(8,128)(2,1)}) %all-gather.6.cloned.1.call-update) | async-done | bytes 4194320 | tf_op jit(solution)/shard_map/all_gather | solution.py:44
  74.2 3.3 %fusion = f32[8,128,128]{2,1,0:T(8,128)S(1)} fusion(bf16[16,8,128,128]{3,2,1,0:T(8,128)(2,1)} %bitcast.46, pred[16]{0:T(512)(128)(4,1)S(1)} %iota_compare_fusion.1), kind=kLoop, calls=%fused_computation.2 | loop fusion | flops 6160384 | bytes 4718608 | tf_op jit(solution)/shard_map/reduce_sum | solution.py:49
  77.6 0.1 copy-done.6
  77.7 3.3 %multiply_reduce_fusion = (f32[1024,8]{0,1:T(8,128)S(1)}, f32[1024,8,128]{2,0,1:T(8,128)S(1)}) fusion(f32[8,128,128]{2,1,0:T(8,128)S(1)} %fusion, bf16[1024,8,128]{0,2,1:T(8,128)(2,1)S(1)} %bitcast.35, f32[512,8,128]{2,0,1:T(8,128)S(1)} %copy-done.5, f32[512,8,128]{2,0,1:T(8,128)S(1)} %copy-done.6), kind=kOutput, calls=%fused_computation.21 | convolution fusion | flops 1614798848 | bytes 11042816 | tf_op jit(solution)/shard_map/thd,hde->the/dot_general | solution.py:50
  81.0 1.4 multiply_convert_fusion
  82.4 2.7 copy.63
  85.2 89.7 %all-gather.4.cloned.1.call-done = bf16[1024,6144]{1,0:T(8,128)(2,1)} async-done(((bf16[1024,384]{1,0:T(8,128)(2,1)}), bf16[1024,6144]{1,0:T(8,128)(2,1)}) %all-gather.4.cloned.1.call-update) | async-done | bytes 12582928 | tf_op jit(solution)/shard_map/all_gather | solution.py:56
  174.9 21.1 %convolution_convert_fusion = bf16[1024,6144]{1,0:T(8,128)(2,1)} fusion(bf16[1024,1024]{0,1:T(8,128)(2,1)} %bitcast.48, bf16[1024,6144]{1,0:T(8,128)(2,1)} %all-gather.4.cloned.1.call-done), kind=kOutput, calls=%fused_computation | convolution fusion | flops 12891193344 | bytes 27262976 | tf_op jit(solution)/shard_map/dot_general | solution.py:58
  195.9 72.1 %reduce-scatter.2.cloned.1.call-done = bf16[128,6144]{1,0:T(8,128)(2,1)} async-done(((bf16[1024,6144]{1,0:T(8,128)(2,1)}), bf16[128,6144]{1,0:T(8,128)(2,1)}) %reduce-scatter.2.cloned.1.call-update) | async-done | bytes 1572880 | tf_op jit(solution)/shard_map/reduce_scatter | solution.py:57
  268.0 2.9 %add_convert_fusion = bf16[128,6144]{1,0:T(8,128)(2,1)} fusion(bf16[128,6144]{1,0:T(8,128)(2,1)S(1)} %copy-done.10, bf16[128,6144]{1,0:T(8,128)(2,1)} %reduce-scatter.2.cloned.1.call-done), kind=kLoop, calls=%fused_computation.26 | loop fusion | flops 3145728 | bytes 4718592 | tf_op jit(solution)/shard_map/convert_element_type | solution.py:63
  (26 shorter events, 0.1 us)
Async XLA Ops:
  6.5 67.7 %all-gather.6.cloned.1.call-start = ((), (), s32[]{:S(2)}) async-start(), calls=%async_computation.3 | async-start | bytes 4456448 | tf_op jit(solution)/shard_map/all_gather | solution.py:44
  9.4 2.4 copy-start.9
  11.8 3.8 %copy-start = (bf16[512,1024]{0,1:T(8,128)(2,1)}, bf16[512,1024]{0,1:T(8,128)(2,1)S(1)}, u32[]{:S(2)}) copy-start(bf16[512,1024]{0,1:T(8,128)(2,1)S(1)} %get-tuple-element.9) | copy-start | bytes 3145732
  13.6 6.3 %copy-start.2 = (bf16[512,1024]{0,1:T(8,128)(2,1)}, bf16[512,1024]{0,1:T(8,128)(2,1)S(1)}, u32[]{:S(2)}) copy-start(bf16[512,1024]{0,1:T(8,128)(2,1)S(1)} %copy.79) | copy-start | bytes 3145732
  16.0 0.8 copy-start.7
  19.2 155.7 %all-gather.4.cloned.1.call-start = ((), (), s32[]{:S(2)}) async-start(), calls=%async_computation.1 | async-start | bytes 13369344 | tf_op jit(solution)/shard_map/all_gather | solution.py:56
  19.9 248.1 %reduce-scatter.2.cloned.1.call-start = ((), (), s32[]{:S(2)}) async-start(), calls=%async_computation.2 | async-start | bytes 14155776 | tf_op jit(solution)/shard_map/reduce_scatter | solution.py:57
  24.0 3.1 %copy-start.4 = (bf16[512,1024]{0,1:T(8,128)(2,1)S(1)}, bf16[512,1024]{0,1:T(8,128)(2,1)}, u32[]{:S(2)}) copy-start(bf16[512,1024]{0,1:T(8,128)(2,1)} %get-tuple-element.10) | copy-start | bytes 3145732
  27.1 1.3 copy-start.3
  28.4 4.6 %copy-start.8 = (f32[8,128,128]{2,1,0:T(8,128)S(1)}, f32[8,128,128]{2,1,0:T(8,128)}, u32[]{:S(2)}) copy-start(f32[8,128,128]{2,1,0:T(8,128)} %copy-done.7) | copy-start | bytes 1572868
  33.0 2.5 copy-start.1
  74.2 3.4 %copy-start.5 = (f32[512,8,128]{2,0,1:T(8,128)S(1)}, f32[512,8,128]{2,0,1:T(8,128)}, u32[]{:S(2)}) copy-start(f32[512,8,128]{2,0,1:T(8,128)} %bitcast_add_fusion) | copy-start | bytes 6291460
  74.2 3.5 %copy-start.6 = (f32[512,8,128]{2,0,1:T(8,128)S(1)}, f32[512,8,128]{2,0,1:T(8,128)}, u32[]{:S(2)}) copy-start(f32[512,8,128]{2,0,1:T(8,128)} %fusion.17) | copy-start | bytes 6291460
  77.7 3.3 %copy-start.11 = (f32[1024]{0:T(1024)S(1)}, f32[1024]{0:T(1024)}, u32[]{:S(2)}) copy-start(f32[1024]{0:T(1024)} %param.9) | copy-start | bytes 12292
  195.9 72.1 %copy-start.10 = (bf16[128,6144]{1,0:T(8,128)(2,1)S(1)}, bf16[128,6144]{1,0:T(8,128)(2,1)}, u32[]{:S(2)}) copy-start(bf16[128,6144]{1,0:T(8,128)(2,1)} %param.11) | copy-start | bytes 4718596
Sparse Core Ops, SparseCore 0:
  19.3 54.8 all-gather.5
  76.3 98.4 all-gather.3
  196.1 71.9 reduce-scatter.1
where the time goes:
time: 278 us; the launch traced here: 277 us
  waiting for transfers between devices  194 us (70%)
  matrix products  42.7 us (15%)
  local copies, waits for them, and re-layouts  15.5 us (6%)
  between operations  13.3 us (5%)
  other arithmetic  11.9 us (4%)
    all_gather x1, waiting for transfers between devices, per_device(): full_weight = lax.all_gather(out_weight, 'seq', axis=1, tiled=True)  89.7 us
    reduce_scatter x1, waiting for transfers between devices, per_device(): lax.psum_scatter(jnp.dot(normed, full_weight, preferred_element_type=jnp....  72.1 us
    all_gather x1, waiting for transfers between devices, per_device(): lax.all_gather(running[None].astype(jnp.bfloat16), 'seq', axis=0, tiled=T...  31.4 us
    dot_general x1, matrix products, per_device(): jnp.dot(normed, full_weight, preferred_element_type=jnp.float32)  21.1 us
    dot_general x2, matrix products, per_device(): jnp.einsum('hts,she->the', scores, v_part.astype(jnp.float32), precision=...  10.5 us
    unnamed x28, local copies, waits for them, and re-layouts  10.2 us
  transfers between devices with their start and end apart: 3, of which 3 were waited for; matrix products, arithmetic and copies ran while one was open for 12% of the time, Pallas kernels for 0%

commit v1 on v0

--- a/solution.py
+++ b/solution.py
@@ -41,9 +41,12 @@
     local_part = jnp.concatenate(pieces, axis=0)
     empty = jnp.zeros((heads, DH, DH), jnp.float32)
     position = lax.axis_index("seq")
-    piece = lax.all_gather(running[None].astype(jnp.bfloat16), "seq", axis=0, tiled=True).astype(
-        jnp.float32
-    )
+    piece = jnp.concatenate(
+        lax.all_to_all(
+            jnp.stack([running[None].astype(jnp.bfloat16)] * lax.axis_size("seq")), "seq", 0, 0
+        ),
+        axis=0,
+    ).astype(jnp.float32)
     ranks = jnp.arange(piece.shape[0], dtype=jnp.int32)
     keep = (ranks < position)[:, None, None, None]
     prefix = empty + jnp.sum(jnp.where(keep, piece, jnp.zeros_like(piece)), axis=0)

time: 278 us -> 259 us (0.932)
  waiting for transfers between devices: 194 us -> 164 us
  starting transfers between devices: 0.08 us -> 8.52 us
    all_to_all x0 -> x1, waiting for transfers between devices: none -> 53.4 us  [per_device(): lax.all_to_all(jnp.stack([running[None].astype(jnp.bfloat16)] * lax.axis_...]
    all_gather x1, waiting for transfers between devices: 89.7 us -> 40.3 us  [per_device(): full_weight = lax.all_gather(out_weight, 'seq', axis=1, tiled=True)]
    all_gather x1 -> x0, waiting for transfers between devices: 31.4 us -> none  [per_device(): lax.all_gather(running[None].astype(jnp.bfloat16), 'seq', axis=0, tiled=T...]
    all_to_all x0 -> x1, starting transfers between devices: none -> 8.48 us  [per_device(): lax.all_to_all(jnp.stack([running[None].astype(jnp.bfloat16)] * lax.axis_...]
    another operation x0 -> x1, local copies, waits for them, and re-layouts: none -> 2.99 us  [per_device(): jnp.stack([running[None].astype(jnp.bfloat16)] * lax.axis_size('seq'))]
  transfers between devices with their start and end apart: 3 -> 3, of which waited for: 3 -> 3; matrix products, arithmetic and copies ran while one was open for 12% -> 18% of each run, Pallas kernels for 0% -> 0%
where the time goes in v1:
time: 259 us
  waiting for transfers between devices  164 us (63%)
  matrix products  40.8 us (16%)
  local copies, waits for them, and re-layouts  17.9 us (7%)
  between operations  13.6 us (5%)
  other arithmetic  13.5 us (5%)
  starting transfers between devices  8.52 us (3%)
    reduce_scatter x1, waiting for transfers between devices, per_device(): lax.psum_scatter(jnp.dot(normed, full_weight, preferred_element_type=jnp....  69.9 us
    all_to_all x1, waiting for transfers between devices, per_device(): lax.all_to_all(jnp.stack([running[None].astype(jnp.bfloat16)] * lax.axis_...  53.4 us
    all_gather x1, waiting for transfers between devices, per_device(): full_weight = lax.all_gather(out_weight, 'seq', axis=1, tiled=True)  40.3 us
    dot_general x1, matrix products, per_device(): jnp.dot(normed, full_weight, preferred_element_type=jnp.float32)  21 us
    dot_general x2, matrix products, per_device(): jnp.einsum('hts,she->the', scores, v_part.astype(jnp.float32), precision=...  10.5 us
    unnamed x28, local copies, waits for them, and re-layouts  10.2 us
    all_to_all x1, starting transfers between devices, per_device(): lax.all_to_all(jnp.stack([running[None].astype(jnp.bfloat16)] * lax.axis_...  8.48 us
    convert_element_type x2, other arithmetic, activate(): return jax.nn.silu(array.astype(jnp.float32)).astype(jnp.bfloat16)  5.7 us
  transfers between devices with their start and end apart: 3, of which 3 were waited for; matrix products, arithmetic and copies ran while one was open for 18% of the time, Pallas kernels for 0%

profile of v1, /device:TPU:1, one launch (start us, length us, event | category | flops | bytes accessed | tf_op | source)
XLA Modules:
  0.0 258.6 jit_solution(5963437819456066050)
XLA Ops:
  6.5 0.7 all-gather.2.cloned.1.call-update
  7.3 3.9 %copy.63 = bf16[1024,1024]{0,1:T(8,128)(2,1)} copy(bf16[1024,1024]{1,0:T(8,128)(2,1)} %param.7) | data formatting | bytes 4194304 | tf_op args[1]
  11.2 1.7 fusion.24
  12.9 0.5 copy.96
  13.5 0.5 copy.95
  14.0 2.8 %fusion.12 = bf16[1024,1024]{0,1:T(8,128)(2,1)S(1)} fusion(bf16[1024,1024]{0,1:T(8,128)(2,1)} %copy.63), kind=kLoop, calls=%fused_computation.18 | loop fusion | flops 6291456 | bytes 4194304 | tf_op jit(solution)/shard_map/convert_element_type | solution.py:10
  16.8 0.2 fusion.25
  17.0 0.4 fusion.28
  17.5 0.5 copy-done.4
  18.0 0.5 copy-done.8
  18.6 0.4 fusion.20
  19.0 3.0 %stack.2 = bf16[16,1,8,128,128]{4,3,2,1,0:T(8,128)(2,1)} broadcast(bf16[8,128,128]{2,1,0:T(8,128)(2,1)S(1)} %fusion.20), dimensions={2,3,4} | broadcast | bytes 4456448 | tf_op jit(solution)/shard_map/stack | solution.py:46
  22.0 8.5 %all-to-all-start = ((bf16[16,1,8,128,128]{4,3,2,1,0:T(8,128)(2,1)}), bf16[16,1,8,128,128]{4,3,2,1,0:T(8,128)(2,1)}, u32[]{:S(2)}, u32[]{:S(2)}) async-start(bf16[16,1,8,128,128]{4,3,2,1,0:T(8,128)(2,1)} %stack.2), calls=%async_computation | async-start | bytes 8388608 | tf_op jit(solution)/shard_map/all_to_all | solution.py:45
  30.5 4.0 %copy.62 = bf16[1024,1024]{0,1:T(8,128)(2,1)} copy(bf16[1024,1024]{1,0:T(8,128)(2,1)} %param.6) | data formatting | bytes 4194304 | tf_op args[0]
  34.5 0.1 iota_compare_fusion
  34.6 2.9 %fusion.8 = bf16[1024,1024]{0,1:T(8,128)(2,1)S(1)} fusion(bf16[1024,1024]{0,1:T(8,128)(2,1)} %copy.62), kind=kLoop, calls=%fused_computation.14 | loop fusion | flops 6291456 | bytes 4194304 | tf_op jit(solution)/shard_map/convert_element_type | solution.py:10
  37.5 0.1 fusion.23
  37.7 1.3 fusion.27
  39.0 4.5 %fusion.1 = f32[8,512,128]{2,1,0:T(8,128)S(1)} fusion(bf16[512,8,128]{0,2,1:T(8,128)(2,1)S(1)} %bitcast.40, f32[8,512,512]{2,1,0:T(8,128)S(1)} %fusion.27, pred[512,512]{1,0:T(8,128)(4,1)S(1)} %iota_compare_fusion), kind=kOutput, calls=%fused_computation.3 | convolution fusion | flops 3223322624 | bytes 11796480 | tf_op jit(solution)/shard_map/hts,she->the/dot_general | solution.py:32
  43.6 2.5 bitcast_add_fusion
  46.1 1.3 fusion.26
  47.4 6.0 %fusion.17 = f32[512,8,128]{2,0,1:T(8,128)} fusion(bf16[512,8,128]{0,2,1:T(8,128)(2,1)S(1)} %bitcast.38, f32[8,512,512]{2,1,0:T(8,128)S(1)} %fusion.26, pred[512,512]{1,0:T(8,128)(4,1)S(1)} %iota_compare_fusion), kind=kOutput, calls=%fused_computation.28 | convolution fusion | flops 3223322624 | bytes 11796480 | tf_op jit(solution)/shard_map/hts,she->the/dot_general | solution.py:32
  53.3 53.4 %all-to-all-done = bf16[16,1,8,128,128]{4,3,2,1,0:T(8,128)(2,1)} async-done(((bf16[16,1,8,128,128]{4,3,2,1,0:T(8,128)(2,1)}), bf16[16,1,8,128,128]{4,3,2,1,0:T(8,128)(2,1)}, u32[]{:S(2)}, u32[]{:S(2)}) %all-to-all-start) | async-done | bytes 4194336 | tf_op jit(solution)/shard_map/all_to_all | solution.py:45
  106.7 3.4 %fusion = f32[8,128,128]{2,1,0:T(8,128)S(1)} fusion(bf16[16,1,8,128,128]{4,3,2,1,0:T(8,128)(2,1)} %all-to-all-done, pred[16]{0:T(512)(128)(4,1)S(1)} %iota_compare_fusion.1), kind=kLoop, calls=%fused_computation.2 | loop fusion | flops 6160384 | bytes 4718608 | tf_op jit(solution)/shard_map/reduce_sum | solution.py:52
  110.1 0.1 copy-done.7
  110.2 3.3 %multiply_reduce_fusion = (f32[1024,8]{0,1:T(8,128)S(1)}, f32[1024,8,128]{2,0,1:T(8,128)S(1)}) fusion(f32[8,128,128]{2,1,0:T(8,128)S(1)} %fusion, bf16[1024,8,128]{0,2,1:T(8,128)(2,1)S(1)} %bitcast.36, f32[512,8,128]{2,0,1:T(8,128)S(1)} %copy-done.6, f32[512,8,128]{2,0,1:T(8,128)S(1)} %copy-done.7), kind=kOutput, calls=%fused_computation.21 | convolution fusion | flops 1614798848 | bytes 11042816 | tf_op jit(solution)/shard_map/thd,hde->the/dot_general | solution.py:53
  113.5 1.4 multiply_convert_fusion
  114.9 2.7 %copy.80 = bf16[1024,8,128]{0,2,1:T(8,128)(2,1)} copy(bf16[1024,8,128]{2,0,1:T(8,128)(2,1)S(1)} %multiply_convert_fusion) | data formatting | bytes 4194304 | tf_op jit(solution)/shard_map/convert_element_type | solution.py:58
  117.6 40.3 %all-gather.2.cloned.1.call-done = bf16[1024,6144]{1,0:T(8,128)(2,1)} async-done(((bf16[1024,384]{1,0:T(8,128)(2,1)}), bf16[1024,6144]{1,0:T(8,128)(2,1)}) %all-gather.2.cloned.1.call-update) | async-done | bytes 12582928 | tf_op jit(solution)/shard_map/all_gather | solution.py:59
  157.9 21.0 %convolution_convert_fusion = bf16[1024,6144]{1,0:T(8,128)(2,1)} fusion(bf16[1024,1024]{0,1:T(8,128)(2,1)} %bitcast.48, bf16[1024,6144]{1,0:T(8,128)(2,1)} %all-gather.2.cloned.1.call-done), kind=kOutput, calls=%fused_computation | convolution fusion | flops 12891193344 | bytes 27262976 | tf_op jit(solution)/shard_map/dot_general | solution.py:61
  179.0 69.9 %reduce-scatter.2.cloned.1.call-done = bf16[128,6144]{1,0:T(8,128)(2,1)} async-done(((bf16[1024,6144]{1,0:T(8,128)(2,1)}), bf16[128,6144]{1,0:T(8,128)(2,1)}) %reduce-scatter.2.cloned.1.call-update) | async-done | bytes 1572880 | tf_op jit(solution)/shard_map/reduce_scatter | solution.py:60
  248.9 2.9 %add_convert_fusion = bf16[128,6144]{1,0:T(8,128)(2,1)} fusion(bf16[128,6144]{1,0:T(8,128)(2,1)S(1)} %copy-done.10, bf16[128,6144]{1,0:T(8,128)(2,1)} %reduce-scatter.2.cloned.1.call-done), kind=kLoop, calls=%fused_computation.26 | loop fusion | flops 3145728 | bytes 4718592 | tf_op jit(solution)/shard_map/convert_element_type | solution.py:66
  (26 shorter events, 0.1 us)
Async XLA Ops:
  6.5 151.4 %all-gather.2.cloned.1.call-start = ((), (), s32[]{:S(2)}) async-start(), calls=%async_computation.2 | async-start | bytes 13369344 | tf_op jit(solution)/shard_map/all_gather | solution.py:59
  13.5 4.0 %copy-start = (bf16[512,1024]{0,1:T(8,128)(2,1)}, bf16[512,1024]{0,1:T(8,128)(2,1)S(1)}, u32[]{:S(2)}) copy-start(bf16[512,1024]{0,1:T(8,128)(2,1)S(1)} %copy.96) | copy-start | bytes 3145732
  17.0 1.0 copy-start.4
  17.0 5.0 %copy-start.2 = (bf16[512,1024]{0,1:T(8,128)(2,1)}, bf16[512,1024]{0,1:T(8,128)(2,1)S(1)}, u32[]{:S(2)}) copy-start(bf16[512,1024]{0,1:T(8,128)(2,1)S(1)} %get-tuple-element.9) | copy-start | bytes 3145732
  17.5 1.1 copy-start.8
  22.0 84.7 %all-to-all-start = ((bf16[16,1,8,128,128]{4,3,2,1,0:T(8,128)(2,1)}), bf16[16,1,8,128,128]{4,3,2,1,0:T(8,128)(2,1)}, u32[]{:S(2)}, u32[]{:S(2)}) async-start(bf16[16,1,8,128,128]{4,3,2,1,0:T(8,128)(2,1)} %stack.2), calls=%async_computation | async-start | bytes 8388608 | tf_op jit(solution)/shard_map/all_to_all | solution.py:45
  30.5 218.4 %reduce-scatter.2.cloned.1.call-start = ((), (), s32[]{:S(2)}) async-start(), calls=%async_computation.3 | async-start | bytes 14155776 | tf_op jit(solution)/shard_map/reduce_scatter | solution.py:60
  34.6 3.1 %copy-start.5 = (bf16[512,1024]{0,1:T(8,128)(2,1)S(1)}, bf16[512,1024]{0,1:T(8,128)(2,1)}, u32[]{:S(2)}) copy-start(bf16[512,1024]{0,1:T(8,128)(2,1)} %copy-done.4) | copy-start | bytes 3145732
  37.7 1.3 copy-start.1
  39.0 4.6 %copy-start.9 = (f32[8,128,128]{2,1,0:T(8,128)S(1)}, f32[8,128,128]{2,1,0:T(8,128)}, u32[]{:S(2)}) copy-start(f32[8,128,128]{2,1,0:T(8,128)} %copy-done.8) | copy-start | bytes 1572868
  43.6 2.5 copy-start.3
  106.7 3.4 %copy-start.6 = (f32[512,8,128]{2,0,1:T(8,128)S(1)}, f32[512,8,128]{2,0,1:T(8,128)}, u32[]{:S(2)}) copy-start(f32[512,8,128]{2,0,1:T(8,128)} %bitcast_add_fusion) | copy-start | bytes 6291460
  106.7 3.5 %copy-start.7 = (f32[512,8,128]{2,0,1:T(8,128)S(1)}, f32[512,8,128]{2,0,1:T(8,128)}, u32[]{:S(2)}) copy-start(f32[512,8,128]{2,0,1:T(8,128)} %fusion.17) | copy-start | bytes 6291460
  110.2 3.3 %copy-start.11 = (f32[1024]{0:T(1024)S(1)}, f32[1024]{0:T(1024)}, u32[]{:S(2)}) copy-start(f32[1024]{0:T(1024)} %param.9) | copy-start | bytes 12292
  178.9 69.9 %copy-start.10 = (bf16[128,6144]{1,0:T(8,128)(2,1)S(1)}, bf16[128,6144]{1,0:T(8,128)(2,1)}, u32[]{:S(2)}) copy-start(bf16[128,6144]{1,0:T(8,128)(2,1)} %param.11) | copy-start | bytes 4718596
Sparse Core Ops, SparseCore 0:
  9.5 148.3 all-gather.1
  179.1 69.7 reduce-scatter.1
